TPU v7x, 32 devices: a whole 2x2x4 slice. The times are simulated.
32 devices in a mesh: epoch: 4 (over z), vel: 8 (over y, x, core).
Axes of the slice: x: 2, y: 2, z: 4, core: 2. Of those that a mesh axis runs over, the one named last changes fastest.
Arguments:
- science: float32 [8, 32, 1024], P('epoch', 'vel'), may hold values from -6 to 6
- variance: float32 [8, 32, 1024], P('epoch', 'vel'), may hold values from 0.25 to 4
- psf: float32 [8, 9], P('epoch'), may hold values from 0.05 to 1
- shifts: int32 [2, 8, 8], P(None, None, 'vel'), may hold values from -16 to 16, as said below
Outputs:
- likelihood: float32 [8, 32, 1024], P('vel', 'epoch')
Inputs may be any that keep to these rules, and one draw needn't show every extreme that they name: For each velocity, the shifts of epoch e are the floor of the velocity's integer rates times the epoch's time over the span of the times; the first epoch's shifts are zero, and times rise with the epoch.
All inputs are finite; a program needn't handle non-finite values.
Results may differ from a plain program's by a relative error of at most 0.0003.
Values sent between devices are 32-bit elements; how exact they have to be, the bound alone decides.
No kernel may reach another device: no remote copies, remote signals or barrier semaphores. Data moves between devices by JAX's collectives and lax.ppermute only.
A program may use at most 64 MiB of HBM per device.

v0:
```python
import jax
import jax.numpy as jnp
from jax import lax
from jax.sharding import PartitionSpec as P

MAXS = 16


def extended(block, sides, width):
    for axis, dim in sides:
        count = lax.axis_size(axis)
        forward = [(i, i + 1) for i in range(count - 1)]
        backward = [(target, source) for source, target in forward]
        low = lax.ppermute(
            lax.slice_in_dim(block, block.shape[dim] - width, None, axis=dim), axis, forward
        )
        high = lax.ppermute(lax.slice_in_dim(block, 0, width, axis=dim), axis, backward)
        block = jnp.concatenate([low, block, high], axis=dim)
    return block


def filter_columns(pairing, weights):
    radius = weights.shape[2] // 2
    breadth = pairing.shape[3]
    padded = jnp.pad(pairing, ((0, 0), (0, 0), (0, 0), (radius, radius)))
    summed = jnp.zeros_like(pairing)
    for offset in range(weights.shape[2]):
        summed = (
            summed + weights[:, :, offset, None, None] * padded[:, :, :, offset : offset + breadth]
        )
    return summed


def filter_rows(rimmed, weights, height):
    summed = jnp.zeros(rimmed.shape[:2] + (height, rimmed.shape[3]), jnp.float32)
    for offset in range(weights.shape[2]):
        summed = (
            summed + weights[:, :, offset, None, None] * rimmed[:, :, offset : offset + height, :]
        )
    return summed


def per_device(science, variance, psf, shifts):
    slots = science.shape[0]
    height = science.shape[1]
    breadth = science.shape[2]
    radius = psf.shape[1] // 2
    pairing = jnp.stack([science / variance, 1.0 / variance], axis=1)
    weights = jnp.stack([psf, psf * psf], axis=1)
    columns_pass = filter_columns(pairing, weights)
    rimmed = extended(columns_pass, (("vel", 2),), radius)
    filtered = filter_rows(rimmed, weights, height)
    local_shifts = lax.dynamic_slice_in_dim(shifts, lax.axis_index("epoch") * slots, slots, 1)
    velocities = shifts.shape[2]
    gathered = lax.all_gather(filtered, "vel", axis=2, tiled=True)
    rows_all = gathered.shape[2]
    padded = jnp.pad(gathered, ((0, 0), (0, 0), (MAXS, MAXS), (MAXS, MAXS)))
    stacks = jnp.zeros((velocities, 2, rows_all, breadth), jnp.float32)
    for epoch_slot in range(slots):
        image = padded[epoch_slot]

        def window_at(shift_col, shift_row):
            return lax.dynamic_slice(
                image, (jnp.int32(0), MAXS + shift_row, MAXS + shift_col), (2, rows_all, breadth)
            )

        stacks = stacks + jax.vmap(window_at)(
            local_shifts[0, epoch_slot], local_shifts[1, epoch_slot]
        )
    mine = lax.psum_scatter(stacks, "epoch", scatter_dimension=2, tiled=True)
    return mine[:, 0] / jnp.sqrt(mine[:, 1])


def solution(mesh):
    return jax.shard_map(
        per_device,
        mesh=mesh,
        in_specs=(
            P("epoch", "vel", None),
            P("epoch", "vel", None),
            P("epoch", None),
            P(None, None, "vel"),
        ),
        out_specs=P("vel", "epoch", None),
        check_vma=False,
    )
```

profile of v0, /device:TPU:0, one launch (start us, length us, event | category | flops | bytes accessed | tf_op | source)
XLA Modules:
  0.0 81.5 jit_solution(1506419152563569825)
XLA Ops:
  6.5 0.0 all-reduce.5.cloned.1.call-start
  6.5 0.7 multiply_bitcast_fusion
  7.2 1.1 %fusion.26 = (f32[2,2,1]{2,0,1:T(2,128)S(1)}, f32[2,2,1]{2,0,1:T(2,128)S(1)}, f32[2,2,1]{2,0,1:T(2,128)S(1)}, f32[2,2,1]{2,0,1:T(2,128)S(1)}, f32[2,2,1]{2,0,1:T...) fusion(f32[2,1,9]{2,0,1:T(2,128)} %bitcast.58, ...), kind=kLoop, calls=%fused_computation.63 | loop fusion | flops 36 | bytes 288 | tf_op jit(solution)/shard_map/stack | solution.py:49
  8.3 0.1 copy.63
  8.4 0.1 copy.64
  8.5 0.1 copy.65
  8.6 0.1 copy.66
  8.7 0.1 copy.67
  8.8 0.1 copy.68
  8.9 0.1 copy.60
  9.0 0.1 copy.61
  9.1 0.1 copy.62
  9.2 0.8 divide_bitcast_fusion.1
  10.0 0.4 multiply_add_fusion
  10.4 2.4 %collective-permute-start = (f32[2,2,4,1024]{3,2,0,1:T(4,128)S(1)}, f32[2,2,4,1024]{3,2,0,1:T(4,128)S(1)}, u32[]{:S(2)}, u32[]{:S(2)}) collective-permute-start(f32[2,2,4,1024]{3,2,0,1:T(4,128)S(1)} %multiply_add_fusion), channel_id=1, source_target_pairs={{0,1},{1,2},{2,3},{3,4},{4,5},{5,6},{6,7},{8,9},{9,10},{10,11},{11... | collective-permute-start | bytes 196616 | tf_op jit(solution)/shard_map/ppermute | solution.py:14
  12.8 1.3 %collective-permute-start.1 = (f32[2,2,4,1024]{3,2,0,1:T(4,128)S(1)}, f32[2,2,4,1024]{3,2,0,1:T(4,128)S(1)}, u32[]{:S(2)}, u32[]{:S(2)}) collective-permute-start(f32[2,2,4,1024]{3,2,0,1:T(4,128)S(1)} %multiply_add_fusion), channel_id=1, source_target_pairs={{1,0},{2,1},{3,2},{4,3},{5,4},{6,5},{7,6},{9,8},{10,9},{11,10},{12... | collective-permute-start | bytes 196616 | tf_op jit(solution)/shard_map/ppermute | solution.py:17
  14.1 1.4 %constant_dynamic-slice_fusion = (s32[1,1,1]{1,2,0:T(1,128)}, s32[1,1,1]{1,2,0:T(1,128)}, s32[1,1,1]{1,2,0:T(1,128)}, s32[1,1,1]{1,2,0:T(1,128)}) fusion(s32[2,8,1]{1,2,0:T(1,128)} %param.7, s32[]{:T(128)S(6)} %select_n.15, s32[]{:T(128)S(6)} %add.166, s32[]{:T(128)S(6)} %add.168), kind=kLoop, calls=%fused_computation.71 | loop fusion | bytes 44 | tf_op jit(solution)/shard_map/slice | solution.py:68
  20.4 0.0 collective-permute-done
  20.5 0.0 collective-permute-done.1
  20.5 0.3 fusion.4
  20.7 0.1 copy.58
  20.8 14.1 %all_gather.3 = f32[2,2,32,1024]{3,1,0,2:T(2,128)S(1)} all-gather(f32[2,2,4,1024]{3,1,0,2:T(2,128)S(1)} %copy.58), channel_id=1, replica_groups=mesh['epoch'=4,'vel'=8] {'vel'}, dimensions={2}, use_global_device_ids=true | all-gather | bytes 589824 | tf_op jit(solution)/shard_map/all_gather | solution.py:55
  34.9 0.7 pad_slice_fusion.1
  35.6 0.0 copy-start
  35.7 1.3 %dynamic-slice_add_fusion = f32[1,2,32,1024]{3,1,0,2:T(2,128)} fusion(f32[1,2,64,1056]{3,1,0,2:T(2,128)S(1)} %get-tuple-element.28, s32[]{:T(128)} %bitcast.30, s32[]{:T(128)} %bitcast.33, f32[1,2,64,1056]{3,1,0,2:T(2,128)S(1)} %get-tuple-element.27, s32[]{:T(128)} %bitcast.24, s32[]{:T(128)} %bitcast.27), kind=kLoop, calls=%fused_computation.2 | loop fusion | flops 65536 | bytes 786448 | tf_op jit(solution)/shard_map/add | solution.py:67
  37.0 0.0 all-reduce.5.cloned.1.call-update
  37.0 0.0 copy-done
  37.0 0.6 dynamic-slice.10
  38.3 34.8 %all-reduce.5.cloned.1.call-done = f32[1,2,32,1024]{3,1,0,2:T(2,128)} async-done(((f32[1,2,32,1024]{3,1,0,2:T(2,128)}), f32[1,2,32,1024]{3,1,0,2:T(2,128)}) %all-reduce.5.cloned.1.call-update) | async-done | bytes 262160
  73.0 1.0 %fusion.24 = f32[1,8,1024]{2,0,1:T(1,128)S(1)} fusion(f32[1,2,32,1024]{3,1,0,2:T(2,128)} %all-reduce.5.cloned.1.call-done, u32[]{:T(128)S(6)} %convert, u32[]{:T(128)S(6)} %multiply.11), kind=kLoop, calls=%fused_computation.45 | loop fusion | flops 8192 | bytes 98312 | tf_op jit(solution)/shard_map/div | solution.py:71
  74.0 0.6 copy.59
  (1 shorter events, 0.0 us)
Async XLA Ops:
  6.5 66.5 %all-reduce.5.cloned.1.call-start = ((), (), s32[]{:S(2)}) async-start(), calls=%async_computation | async-start | bytes 524288
  10.4 10.0 %collective-permute-start = (f32[2,2,4,1024]{3,2,0,1:T(4,128)S(1)}, f32[2,2,4,1024]{3,2,0,1:T(4,128)S(1)}, u32[]{:S(2)}, u32[]{:S(2)}) collective-permute-start(f32[2,2,4,1024]{3,2,0,1:T(4,128)S(1)} %multiply_add_fusion), channel_id=1, source_target_pairs={{0,1},{1,2},{2,3},{3,4},{4,5},{5,6},{6,7},{8,9},{9,10},{10,11},{11... | collective-permute-start | bytes 196616 | tf_op jit(solution)/shard_map/ppermute | solution.py:14
  12.8 7.6 %collective-permute-start.1 = (f32[2,2,4,1024]{3,2,0,1:T(4,128)S(1)}, f32[2,2,4,1024]{3,2,0,1:T(4,128)S(1)}, u32[]{:S(2)}, u32[]{:S(2)}) collective-permute-start(f32[2,2,4,1024]{3,2,0,1:T(4,128)S(1)} %multiply_add_fusion), channel_id=1, source_target_pairs={{1,0},{2,1},{3,2},{4,3},{5,4},{6,5},{7,6},{9,8},{10,9},{11,10},{12... | collective-permute-start | bytes 196616 | tf_op jit(solution)/shard_map/ppermute | solution.py:17
  35.6 1.4 %copy-start = (u32[32]{0:T(128)S(1)}, u32[32]{0:T(128)}, u32[]{:S(2)}) copy-start(u32[32]{0:T(128)} %constant.89) | copy-start | bytes 388
Sparse Core Ops, SparseCore 0:
  37.1 35.8 all-reduce.4
where the time goes:
time: 81.9 us; the launch traced here: 81.5 us
  waiting for transfers between devices  34.8 us (42%)
  between operations  19.1 us (23%)
  blocking collectives  14.1 us (17%)
  other arithmetic  5.5 us (7%)
  local copies, waits for them, and re-layouts  4.27 us (5%)
  starting transfers between devices  3.69 us (5%)
    unnamed x2, waiting for transfers between devices  34.8 us
    all_gather x1, blocking collectives, per_device(): gathered = lax.all_gather(filtered, 'vel', axis=2, tiled=True)  14.1 us
    ppermute x1, starting transfers between devices, extended(): lax.ppermute(lax.slice_in_dim(block, block.shape[dim] - width, None, axis...  2.4 us
    another operation x2, other arithmetic, per_device(): weights = jnp.stack([psf, psf * psf], axis=1)  1.77 us
  transfers between devices with their start and end apart: 3, of which 1 were waited for; matrix products, arithmetic and copies ran while one was open for 2% of the time, Pallas kernels for 0%

commit v1 on v0

--- a/solution.py
+++ b/solution.py
@@ -52,7 +52,12 @@
     filtered = filter_rows(rimmed, weights, height)
     local_shifts = lax.dynamic_slice_in_dim(shifts, lax.axis_index("epoch") * slots, slots, 1)
     velocities = shifts.shape[2]
-    gathered = lax.all_gather(filtered, "vel", axis=2, tiled=True)
+    ring = [filtered]
+    for hop in range(7):
+        ring.append(lax.ppermute(ring[-1], "vel", [(dev, (dev + 1) % 8) for dev in range(8)]))
+    gathered = jnp.roll(
+        jnp.concatenate(ring[::-1], axis=2), (lax.axis_index("vel") + 1) * ring[0].shape[2], axis=2
+    )
     rows_all = gathered.shape[2]
     padded = jnp.pad(gathered, ((0, 0), (0, 0), (MAXS, MAXS), (MAXS, MAXS)))
     stacks = jnp.zeros((velocities, 2, rows_all, breadth), jnp.float32)

time: 81.9 us -> 86.9 us (1.061)
  waiting for transfers between devices: 34.8 us -> 52.5 us
  blocking collectives: 14.1 us -> 0 us
  starting transfers between devices: 3.69 us -> 6.7 us
  local copies, waits for them, and re-layouts: 4.27 us -> 3.05 us
    unnamed x2 -> x1, waiting for transfers between devices: 34.8 us -> 0.02 us
    ppermute x0 -> x7, waiting for transfers between devices: none -> 24.6 us  [per_device(): lax.ppermute(ring[-1], 'vel', [(dev, (dev + 1) % 8) for dev in range(8)])]
    reduce_scatter x0 -> x1, waiting for transfers between devices: none -> 23.9 us  [per_device(): mine = lax.psum_scatter(stacks, 'epoch', scatter_dimension=2, tiled=True)]
    all_gather x1 -> x0, blocking collectives: 14.1 us -> none  [per_device(): gathered = lax.all_gather(filtered, 'vel', axis=2, tiled=True)]
    ppermute x1, waiting for transfers between devices: 0.01 us -> 3.93 us  [extended(): lax.ppermute(lax.slice_in_dim(block, 0, width, axis=dim), axis, backward)]
    ppermute x0 -> x7, starting transfers between devices: none -> 3 us  [per_device(): lax.ppermute(ring[-1], 'vel', [(dev, (dev + 1) % 8) for dev in range(8)])]
    slice x0 -> x9, local copies, waits for them, and re-layouts: none -> 0.88 us  [the longest x8 0.78 us: filter_columns(): weights[:, :, offset, None, None] * padded[:, :, :, offset:offset + breadth]]
    mul x9 -> x0, local copies, waits for them, and re-layouts: 0.88 us -> none  [the longest x8 0.78 us: filter_columns(): weights[:, :, offset, None, None] * padded[:, :, :, offset:offset + breadth]]
  transfers between devices with their start and end apart: 3 -> 10, of which waited for: 1 -> 8; matrix products, arithmetic and copies ran while one was open for 2% -> 2% of each run, Pallas kernels for 0% -> 0%
where the time goes in v1:
time: 86.9 us; the launch traced here: 86.5 us
  waiting for transfers between devices  52.5 us (60%)
  between operations  18.7 us (22%)
  starting transfers between devices  6.7 us (8%)
  other arithmetic  5.53 us (6%)
  local copies, waits for them, and re-layouts  3.05 us (4%)
    ppermute x7, waiting for transfers between devices, per_device(): lax.ppermute(ring[-1], 'vel', [(dev, (dev + 1) % 8) for dev in range(8)])  24.6 us
    reduce_scatter x1, waiting for transfers between devices, per_device(): mine = lax.psum_scatter(stacks, 'epoch', scatter_dimension=2, tiled=True)  23.9 us
    ppermute x1, waiting for transfers between devices, extended(): lax.ppermute(lax.slice_in_dim(block, 0, width, axis=dim), axis, backward)  3.93 us
    ppermute x7, starting transfers between devices, per_device(): lax.ppermute(ring[-1], 'vel', [(dev, (dev + 1) % 8) for dev in range(8)])  3 us
    ppermute x1, starting transfers between devices, extended(): lax.ppermute(lax.slice_in_dim(block, block.shape[dim] - width, None, axis...  2.4 us
    another operation x2, other arithmetic, per_device(): weights = jnp.stack([psf, psf * psf], axis=1)  1.77 us
  transfers between devices with their start and end apart: 10, of which 8 were waited for; matrix products, arithmetic and copies ran while one was open for 2% of the time, Pallas kernels for 0%

profile of v1, /device:TPU:0, one launch (start us, length us, event | category | flops | bytes accessed | tf_op | source)
XLA Modules:
  0.0 86.5 jit_solution(8333634695265740697)
XLA Ops:
  6.5 0.7 multiply_bitcast_fusion
  7.2 1.1 %fusion.26 = (f32[2,2,1]{2,0,1:T(2,128)S(1)}, f32[2,2,1]{2,0,1:T(2,128)S(1)}, f32[2,2,1]{2,0,1:T(2,128)S(1)}, f32[2,2,1]{2,0,1:T(2,128)S(1)}, f32[2,2,1]{2,0,1:T...) fusion(f32[2,1,9]{2,0,1:T(2,128)} %bitcast.48, ...), kind=kLoop, calls=%fused_computation.63 | loop fusion | flops 36 | bytes 288 | tf_op jit(solution)/shard_map/stack | solution.py:49
  8.3 0.1 copy.11
  8.4 0.1 copy.12
  8.5 0.1 copy.13
  8.6 0.1 copy.5
  8.7 0.1 copy.6
  8.8 0.1 copy.7
  8.9 0.1 copy.8
  9.0 0.1 copy.9
  9.1 0.1 copy.10
  9.2 0.8 divide_bitcast_fusion.1
  10.0 0.4 multiply_add_fusion
  10.4 2.4 %collective-permute-start = (f32[2,2,4,1024]{3,2,1,0:T(4,128)S(1)}, f32[2,2,4,1024]{3,2,1,0:T(4,128)S(1)}, u32[]{:S(2)}, u32[]{:S(2)}) collective-permute-start(f32[2,2,4,1024]{3,2,1,0:T(4,128)S(1)} %multiply_add_fusion), channel_id=1, source_target_pairs={{0,1},{1,2},{2,3},{3,4},{4,5},{5,6},{6,7},{8,9},{9,10},{10,11},{11... | collective-permute-start | bytes 196616 | tf_op jit(solution)/shard_map/ppermute | solution.py:14
  12.8 1.3 %collective-permute-start.1 = (f32[2,2,4,1024]{3,2,1,0:T(4,128)S(1)}, f32[2,2,4,1024]{3,2,1,0:T(4,128)S(1)}, u32[]{:S(2)}, u32[]{:S(2)}) collective-permute-start(f32[2,2,4,1024]{3,2,1,0:T(4,128)S(1)} %multiply_add_fusion), channel_id=1, source_target_pairs={{1,0},{2,1},{3,2},{4,3},{5,4},{6,5},{7,6},{9,8},{10,9},{11,10},{12... | collective-permute-start | bytes 196616 | tf_op jit(solution)/shard_map/ppermute | solution.py:17
  14.1 3.9 %collective-permute-done.1 = f32[2,2,4,1024]{3,2,1,0:T(4,128)S(1)} collective-permute-done((f32[2,2,4,1024]{3,2,1,0:T(4,128)S(1)}, f32[2,2,4,1024]{3,2,1,0:T(4,128)S(1)}, u32[]{:S(2)}, u32[]{:S(2)}) %collective-permute-start.1) | collective-permute-done | bytes 65568 | tf_op jit(solution)/shard_map/ppermute | solution.py:17
  18.1 0.3 fusion.4
  18.3 3.0 %collective-permute-start.2 = (f32[2,2,4,1024]{3,2,1,0:T(4,128)S(1)}, f32[2,2,4,1024]{3,2,1,0:T(4,128)S(1)}, u32[]{:S(2)}, u32[]{:S(2)}) collective-permute-start(f32[2,2,4,1024]{3,2,1,0:T(4,128)S(1)} %fusion.4), channel_id=1, source_target_pairs={{0,1},{1,2},{2,3},{3,4},{4,5},{5,6},{6,7},{7,0},{8,9},{9,10},{10,1... | collective-permute-start | bytes 196616 | tf_op jit(solution)/shard_map/ppermute | solution.py:57
  21.3 1.7 %collective-permute-done.2 = f32[2,2,4,1024]{3,2,1,0:T(4,128)S(1)} collective-permute-done((f32[2,2,4,1024]{3,2,1,0:T(4,128)S(1)}, f32[2,2,4,1024]{3,2,1,0:T(4,128)S(1)}, u32[]{:S(2)}, u32[]{:S(2)}) %collective-permute-start.2) | collective-permute-done | bytes 65568 | tf_op jit(solution)/shard_map/ppermute | solution.py:57
  23.0 4.6 %collective-permute-done.3 = f32[2,2,4,1024]{3,2,1,0:T(4,128)S(1)} collective-permute-done((f32[2,2,4,1024]{3,2,1,0:T(4,128)S(1)}, f32[2,2,4,1024]{3,2,1,0:T(4,128)S(1)}, u32[]{:S(2)}, u32[]{:S(2)}) %collective-permute-start.3) | collective-permute-done | bytes 65568 | tf_op jit(solution)/shard_map/ppermute | solution.py:57
  27.5 4.6 %collective-permute-done.4 = f32[2,2,4,1024]{3,2,1,0:T(4,128)S(1)} collective-permute-done((f32[2,2,4,1024]{3,2,1,0:T(4,128)S(1)}, f32[2,2,4,1024]{3,2,1,0:T(4,128)S(1)}, u32[]{:S(2)}, u32[]{:S(2)}) %collective-permute-start.4) | collective-permute-done | bytes 65568 | tf_op jit(solution)/shard_map/ppermute | solution.py:57
  32.1 4.6 %collective-permute-done.5 = f32[2,2,4,1024]{3,2,1,0:T(4,128)S(1)} collective-permute-done((f32[2,2,4,1024]{3,2,1,0:T(4,128)S(1)}, f32[2,2,4,1024]{3,2,1,0:T(4,128)S(1)}, u32[]{:S(2)}, u32[]{:S(2)}) %collective-permute-start.5) | collective-permute-done | bytes 65568 | tf_op jit(solution)/shard_map/ppermute | solution.py:57
  36.7 4.6 %collective-permute-done.6 = f32[2,2,4,1024]{3,2,1,0:T(4,128)S(1)} collective-permute-done((f32[2,2,4,1024]{3,2,1,0:T(4,128)S(1)}, f32[2,2,4,1024]{3,2,1,0:T(4,128)S(1)}, u32[]{:S(2)}, u32[]{:S(2)}) %collective-permute-start.6) | collective-permute-done | bytes 65568 | tf_op jit(solution)/shard_map/ppermute | solution.py:57
  41.3 4.6 %collective-permute-done.7 = f32[2,2,4,1024]{3,2,1,0:T(4,128)S(1)} collective-permute-done((f32[2,2,4,1024]{3,2,1,0:T(4,128)S(1)}, f32[2,2,4,1024]{3,2,1,0:T(4,128)S(1)}, u32[]{:S(2)}, u32[]{:S(2)}) %collective-permute-start.7) | collective-permute-done | bytes 65568 | tf_op jit(solution)/shard_map/ppermute | solution.py:57
  45.9 1.4 %constant_dynamic-slice_fusion = (s32[1,1,1]{1,2,0:T(1,128)}, s32[1,1,1]{1,2,0:T(1,128)}, s32[1,1,1]{1,2,0:T(1,128)}, s32[1,1,1]{1,2,0:T(1,128)}) fusion(s32[2,8,1]{1,2,0:T(1,128)} %param.7, s32[]{:T(128)S(6)} %select_n.30, s32[]{:T(128)S(6)} %add.180, s32[]{:T(128)S(6)} %add.182), kind=kLoop, calls=%fused_computation.71 | loop fusion | bytes 44 | tf_op jit(solution)/shard_map/slice | solution.py:73
  52.5 0.5 concatenate.25
  53.0 0.1 constant_dynamic-slice_fusion.4
  53.1 0.2 pad_slice_fusion.1
  53.3 0.9 %dynamic-slice_add_fusion = f32[1,2,32,1024]{3,2,1,0:T(8,128)} fusion(f32[1,2,64,1056]{3,2,1,0:T(8,128)S(1)} %get-tuple-element.28, s32[]{:T(128)} %bitcast.21, s32[]{:T(128)} %bitcast.24, f32[1,2,64,1056]{3,2,1,0:T(8,128)S(1)} %get-tuple-element.27, s32[]{:T(128)} %bitcast.15, s32[]{:T(128)} %bitcast.18), kind=kLoop, calls=%fused_computation.2 | loop fusion | flops 65536 | bytes 786448 | tf_op jit(solution)/shard_map/add | solution.py:72
  54.2 0.0 reduce-scatter.2.cloned.1.call-update
  54.3 23.9 %reduce-scatter.2.cloned.1.call-done = f32[1,2,8,1024]{3,2,1,0:T(8,128)} async-done(((f32[1,2,32,1024]{3,2,1,0:T(8,128)}), f32[1,2,8,1024]{3,2,1,0:T(8,128)}) %reduce-scatter.2.cloned.1.call-update) | async-done | bytes 65552 | tf_op jit(solution)/shard_map/reduce_scatter | solution.py:75
  78.2 1.4 %fusion.24 = f32[1,8,1024]{2,1,0:T(8,128)} fusion(f32[1,2,8,1024]{3,2,1,0:T(8,128)} %reduce-scatter.2.cloned.1.call-done), kind=kLoop, calls=%fused_computation.43 | loop fusion | flops 8192 | bytes 98304 | tf_op jit(solution)/shard_map/div | solution.py:76
  (10 shorter events, 0.0 us)
Async XLA Ops:
  6.5 71.7 %reduce-scatter.2.cloned.1.call-start = ((), (), s32[]{:S(2)}) async-start(), calls=%async_computation.1 | async-start | bytes 327680 | tf_op jit(solution)/shard_map/reduce_scatter | solution.py:75
  10.4 3.7 %collective-permute-start = (f32[2,2,4,1024]{3,2,1,0:T(4,128)S(1)}, f32[2,2,4,1024]{3,2,1,0:T(4,128)S(1)}, u32[]{:S(2)}, u32[]{:S(2)}) collective-permute-start(f32[2,2,4,1024]{3,2,1,0:T(4,128)S(1)} %multiply_add_fusion), channel_id=1, source_target_pairs={{0,1},{1,2},{2,3},{3,4},{4,5},{5,6},{6,7},{8,9},{9,10},{10,11},{11... | collective-permute-start | bytes 196616 | tf_op jit(solution)/shard_map/ppermute | solution.py:14
  12.8 5.2 %collective-permute-start.1 = (f32[2,2,4,1024]{3,2,1,0:T(4,128)S(1)}, f32[2,2,4,1024]{3,2,1,0:T(4,128)S(1)}, u32[]{:S(2)}, u32[]{:S(2)}) collective-permute-start(f32[2,2,4,1024]{3,2,1,0:T(4,128)S(1)} %multiply_add_fusion), channel_id=1, source_target_pairs={{1,0},{2,1},{3,2},{4,3},{5,4},{6,5},{7,6},{9,8},{10,9},{11,10},{12... | collective-permute-start | bytes 196616 | tf_op jit(solution)/shard_map/ppermute | solution.py:17
  18.3 4.6 %collective-permute-start.2 = (f32[2,2,4,1024]{3,2,1,0:T(4,128)S(1)}, f32[2,2,4,1024]{3,2,1,0:T(4,128)S(1)}, u32[]{:S(2)}, u32[]{:S(2)}) collective-permute-start(f32[2,2,4,1024]{3,2,1,0:T(4,128)S(1)} %fusion.4), channel_id=1, source_target_pairs={{0,1},{1,2},{2,3},{3,4},{4,5},{5,6},{6,7},{7,0},{8,9},{9,10},{10,1... | collective-permute-start | bytes 196616 | tf_op jit(solution)/shard_map/ppermute | solution.py:57
  23.0 4.6 %collective-permute-start.3 = (f32[2,2,4,1024]{3,2,1,0:T(4,128)S(1)}, f32[2,2,4,1024]{3,2,1,0:T(4,128)S(1)}, u32[]{:S(2)}, u32[]{:S(2)}) collective-permute-start(f32[2,2,4,1024]{3,2,1,0:T(4,128)S(1)} %collective-permute-done.2), channel_id=1, source_target_pairs={{0,1},{1,2},{2,3},{3,4},{4,5},{5,6},{6,7},{7,0},{8,9},{9,10},{10,1... | collective-permute-start | bytes 196616 | tf_op jit(solution)/shard_map/ppermute | solution.py:57
  27.5 4.6 %collective-permute-start.4 = (f32[2,2,4,1024]{3,2,1,0:T(4,128)S(1)}, f32[2,2,4,1024]{3,2,1,0:T(4,128)S(1)}, u32[]{:S(2)}, u32[]{:S(2)}) collective-permute-start(f32[2,2,4,1024]{3,2,1,0:T(4,128)S(1)} %collective-permute-done.3), channel_id=1, source_target_pairs={{0,1},{1,2},{2,3},{3,4},{4,5},{5,6},{6,7},{7,0},{8,9},{9,10},{10,1... | collective-permute-start | bytes 196616 | tf_op jit(solution)/shard_map/ppermute | solution.py:57
  32.1 4.6 %collective-permute-start.5 = (f32[2,2,4,1024]{3,2,1,0:T(4,128)S(1)}, f32[2,2,4,1024]{3,2,1,0:T(4,128)S(1)}, u32[]{:S(2)}, u32[]{:S(2)}) collective-permute-start(f32[2,2,4,1024]{3,2,1,0:T(4,128)S(1)} %collective-permute-done.4), channel_id=1, source_target_pairs={{0,1},{1,2},{2,3},{3,4},{4,5},{5,6},{6,7},{7,0},{8,9},{9,10},{10,1... | collective-permute-start | bytes 196616 | tf_op jit(solution)/shard_map/ppermute | solution.py:57
  36.7 4.6 %collective-permute-start.6 = (f32[2,2,4,1024]{3,2,1,0:T(4,128)S(1)}, f32[2,2,4,1024]{3,2,1,0:T(4,128)S(1)}, u32[]{:S(2)}, u32[]{:S(2)}) collective-permute-start(f32[2,2,4,1024]{3,2,1,0:T(4,128)S(1)} %collective-permute-done.5), channel_id=1, source_target_pairs={{0,1},{1,2},{2,3},{3,4},{4,5},{5,6},{6,7},{7,0},{8,9},{9,10},{10,1... | collective-permute-start | bytes 196616 | tf_op jit(solution)/shard_map/ppermute | solution.py:57
  41.3 4.6 %collective-permute-start.7 = (f32[2,2,4,1024]{3,2,1,0:T(4,128)S(1)}, f32[2,2,4,1024]{3,2,1,0:T(4,128)S(1)}, u32[]{:S(2)}, u32[]{:S(2)}) collective-permute-start(f32[2,2,4,1024]{3,2,1,0:T(4,128)S(1)} %collective-permute-done.6), channel_id=1, source_target_pairs={{0,1},{1,2},{2,3},{3,4},{4,5},{5,6},{6,7},{7,0},{8,9},{9,10},{10,1... | collective-permute-start | bytes 196616 | tf_op jit(solution)/shard_map/ppermute | solution.py:57
  45.9 6.6 %collective-permute-start.8 = (f32[2,2,4,1024]{3,2,1,0:T(4,128)S(1)}, f32[2,2,4,1024]{3,2,1,0:T(4,128)S(1)}, u32[]{:S(2)}, u32[]{:S(2)}) collective-permute-start(f32[2,2,4,1024]{3,2,1,0:T(4,128)S(1)} %collective-permute-done.7), channel_id=1, source_target_pairs={{0,1},{1,2},{2,3},{3,4},{4,5},{5,6},{6,7},{7,0},{8,9},{9,10},{10,1... | collective-permute-start | bytes 196616 | tf_op jit(solution)/shard_map/ppermute | solution.py:57
Sparse Core Ops, SparseCore 0:
  54.4 23.7 reduce-scatter.1
